TPU v7x, 512 devices: a whole 4x8x8 slice. The times are simulated.
512 devices in a mesh: shard: 128 (over y, z, core), tensor: 4 (over x).
Axes of the slice: x: 4, y: 8, z: 8, core: 2. Of those that a mesh axis runs over, the one named last changes fastest.
Arguments:
- grad_query: bfloat16 [128, 1024, 512], P('shard', None, 'tensor'), may hold values from -8 to 8
- error_query: float32 [128, 1024, 512], P('shard', None, 'tensor'), may hold values from -3 to 3
- grad_output: bfloat16 [128, 512, 1024], P('shard', 'tensor'), may hold values from -8 to 8
- error_output: float32 [128, 512, 1024], P('shard', 'tensor'), may hold values from -3 to 3
- start_query: float32 [512, 32], P('tensor'), may hold values from -6 to 6
- start_output: float32 [1024, 32], replicated, may hold values from -6 to 6
- weight_query: float32 [1024, 512], P('shard', 'tensor'), may hold values from -0.1875 to 0.1875
- weight_output: float32 [512, 1024], P('tensor', 'shard'), may hold values from -0.25 to 0.25
- moment_query: float32 [1024, 512], P('shard', 'tensor'), may hold values from -1.2 to 1.2
- moment_output: float32 [512, 1024], P('tensor', 'shard'), may hold values from -1.2 to 1.2
- grad_vector: bfloat16 [128, 3584], P('shard'), may hold values from -12 to 12
- moment_vector: float32 [3584], P('shard'), may hold values from -1.2 to 1.2
- weight_vector: float32 [3584], P('shard'), may hold values from 0.5 to 1.5
Outputs:
- new_error_query: float32 [128, 1024, 512], P('shard', None, 'tensor')
- new_error_output: float32 [128, 512, 1024], P('shard', 'tensor')
- new_moment_query: float32 [1024, 512], P('shard', 'tensor')
- new_moment_output: float32 [512, 1024], P('tensor', 'shard')
- new_weight_query: float32 [1024, 512], P(None, 'tensor')
- new_weight_output: float32 [512, 1024], P('tensor')
- new_moment_vector: float32 [3584], P('shard')
- new_weight_vector: float32 [3584], replicated
All inputs are finite; a program needn't handle non-finite values.
Results may differ from a plain program's by a relative error of at most 0.0003.
Values sent between devices are 32-bit elements; how exact they have to be, the bound alone decides.
No kernel may reach another device: no remote copies, remote signals or barrier semaphores. Data moves between devices by JAX's collectives and lax.ppermute only.
A program may use at most 64 MiB of HBM per device.

v0:
```python
import jax
import jax.numpy as jnp
from jax import lax
from jax.sharding import PartitionSpec as P

ROUNDS = 2
highest = lax.Precision.HIGHEST


def product(left, right):
    return jnp.dot(left, right, precision=highest, preferred_element_type=jnp.float32)


def product_inner(left, right):
    return lax.dot_general(
        left, right, (((0,), (0,)), ((), ())), precision=highest, preferred_element_type=jnp.float32
    )


def solve_rows(gram, factor):
    lower = jnp.linalg.cholesky(gram)
    return jax.scipy.linalg.solve_triangular(lower, factor.T, lower=True).T


def orthonormal(factor):
    return solve_rows(product_inner(factor, factor), factor)


def orthonormal_rows(factor):
    gram = lax.psum(product_inner(factor, factor), "tensor")
    return solve_rows(gram, factor)


def local(
    grad_query,
    error_query,
    grad_output,
    error_output,
    start_query,
    start_output,
    weight_query,
    weight_output,
    moment_query,
    moment_output,
    grad_vector,
    moment_vector,
    weight_vector,
):
    replicas = lax.axis_size("shard")
    shard_index = lax.axis_index("shard")
    total_query = grad_query[0].astype(jnp.float32) + error_query[0]
    total_output = grad_output[0].astype(jnp.float32) + error_output[0]
    factor_query = start_query
    factor_output = start_output
    for turn in range(ROUNDS):
        part_query = product(total_query, factor_query)
        part_output = product(total_output, factor_output)
        sum_query = lax.psum(part_query, ("shard", "tensor"))
        sum_output = lax.psum(part_output, "shard")
        left_query = orthonormal(sum_query)
        left_output = orthonormal_rows(sum_output)
        right_query_part = product_inner(total_query, left_query)
        right_output_part = product_inner(total_output, left_output)
        factor_query = lax.psum(right_query_part, "shard")
        factor_output = lax.psum(right_output_part, ("shard", "tensor"))
    approx_query = product(left_query, factor_query.T) / replicas
    approx_output = product(left_output, factor_output.T) / replicas
    new_error_query = (total_query - approx_query)[None]
    new_error_output = (total_output - approx_output)[None]
    rows_block = moment_query.shape[0]
    block_query = lax.dynamic_slice_in_dim(approx_query, shard_index * rows_block, rows_block, 0)
    cols_block = moment_output.shape[1]
    block_output = lax.dynamic_slice_in_dim(approx_output, shard_index * cols_block, cols_block, 1)
    new_moment_query = 0.9 * moment_query + block_query
    new_moment_output = 0.9 * moment_output + block_output
    stepped_query = weight_query - 0.01 * new_moment_query
    stepped_output = weight_output - 0.01 * new_moment_output
    local_vector = grad_vector[0].astype(jnp.float32)
    vector_block = moment_vector.shape[0]
    vector_whole = lax.psum(local_vector, "shard")
    vector_part = lax.dynamic_slice_in_dim(
        vector_whole, shard_index * vector_block, vector_block, 0
    )
    vector_mean = vector_part / replicas
    new_moment_vector = 0.9 * moment_vector + vector_mean
    stepped_vector = weight_vector - 0.01 * new_moment_vector
    new_weight_query, new_weight_output, new_weight_vector = (
        lax.all_gather(stepped_query, "shard", axis=0, tiled=True),
        lax.all_gather(stepped_output, "shard", axis=1, tiled=True),
        lax.all_gather(stepped_vector, "shard", axis=0, tiled=True),
    )
    return (
        new_error_query,
        new_error_output,
        new_moment_query,
        new_moment_output,
        new_weight_query,
        new_weight_output,
        new_moment_vector,
        new_weight_vector,
    )


def solution(mesh):
    in_specs = (
        P("shard", None, "tensor"),
        P("shard", None, "tensor"),
        P("shard", "tensor", None),
        P("shard", "tensor", None),
        P("tensor", None),
        P(),
        P("shard", "tensor"),
        P("tensor", "shard"),
        P("shard", "tensor"),
        P("tensor", "shard"),
        P("shard", None),
        P("shard"),
        P("shard"),
    )
    out_specs = (
        P("shard", None, "tensor"),
        P("shard", "tensor", None),
        P("shard", "tensor"),
        P("tensor", "shard"),
        P(None, "tensor"),
        P("tensor", None),
        P("shard"),
        P(),
    )
    return jax.shard_map(local, mesh=mesh, in_specs=in_specs, out_specs=out_specs, check_vma=False)
```

profile of v0, /device:TPU:1, one launch (start us, length us, event | category | flops | bytes accessed | tf_op | source)
XLA Modules:
  0.0 2203.4 jit_solution(7634404734054702130)
XLA Ops:
  7.2 1.2 copy.45
  8.6 0.4 fusion.6
  9.1 498.1 %psum.81 = f32[128,32]{0,1:T(8,128)S(1)} all-reduce(f32[128,32]{0,1:T(8,128)S(1)} %fusion.6), channel_id=1, replica_groups=mesh['shard'=128,'tensor'=4] {'shard'}, use_global_device_ids=true, to_apply=%region_6.9 | all-reduce | flops 4096 | bytes 32768 | tf_op jit(solution)/shard_map/psum | solution.py:59
  507.3 13.2 psum.82
  520.6 2.9 cholesky.96
  523.6 0.6 compare_reduce_fusion.1
  524.2 0.7 fusion.24
  524.9 2.4 custom-call.12
  527.6 1.3 fusion.4
  528.9 1.3 fusion.15
  530.3 1.3 dynamic-slice
  532.3 265.7 %all-reduce.10.cloned.1.call-done = (f32[1024,32]{0,1:T(8,128)}, f32[1024,32]{0,1:T(8,128)}) async-done(((f32[1024,32]{0,1:T(8,128)}, f32[1024,32]{0,1:T(8,128)}), (f32[1024,32]{0,1:T(8,128)}, f32[1024,32]{0,1:T(8,128)})) %all-reduce.10.cloned.1.call-update) | async-done | bytes 262160 | tf_op jit(solution)/shard_map/psum | solution.py:58
  798.0 1.4 fusion.2
  799.7 2.9 cholesky.74
  802.7 0.6 compare_reduce_fusion.3
  803.3 0.7 fusion.22
  804.0 2.4 custom-call.10
  806.4 0.3 fusion.20
  806.8 0.4 fusion.13
  807.2 487.8 %all-reduce.4 = (f32[128,32]{0,1:T(8,128)S(1)}, f32[128,32]{0,1:T(8,128)S(1)}, f32[3584]{0:T(1024)S(1)}) all-reduce(f32[128,32]{0,1:T(8,128)S(1)} %fusion.13, f32[128,32]{0,1:T(8,128)S(1)} %fusion.2, f32[3584]{0:T(1024)S(1)} %convert_reduce_fusion), channel_id=1, replica_groups=mesh['shard'=128,'tensor'=4] {'shard'}, use_global_device_ids=true, to_apply=%region_3.6 | all-reduce | flops 11776 | bytes 94208 | tf_op jit(solution)/shard_map/psum | solution.py:64
  1295.2 12.4 psum.85
  1307.6 2.9 cholesky.107
  1310.6 0.6 compare_reduce_fusion
  1311.2 0.7 fusion.25
  1311.9 2.4 custom-call.13
  1314.6 1.3 fusion.11
  1315.9 1.3 fusion
  1317.3 0.6 copy-done.13
  1317.9 0.6 subtract_dynamic-update-slice_fusion
  1318.5 270.5 %all-reduce.8.cloned.1.call-done = (f32[1024,32]{0,1:T(8,128)}, f32[1024,32]{0,1:T(8,128)}) async-done(((f32[1024,32]{0,1:T(8,128)}, f32[1024,32]{0,1:T(8,128)}), (f32[1024,32]{0,1:T(8,128)}, f32[1024,32]{0,1:T(8,128)})) %all-reduce.8.cloned.1.call-update) | async-done | bytes 262160 | tf_op jit(solution)/shard_map/psum | solution.py:58
  1589.0 1.2 fusion.41
  1590.3 2.9 cholesky.85
  1593.3 0.6 compare_reduce_fusion.2
  1593.9 0.7 fusion.23
  1594.6 2.4 custom-call.11
  1597.0 0.3 fusion.18
  1597.4 0.4 fusion.9
  1597.8 487.8 %all-reduce.3 = (f32[128,32]{0,1:T(8,128)S(1)}, f32[3584]{0:T(1024)}) all-reduce(f32[128,32]{0,1:T(8,128)S(1)} %fusion.9, f32[3584]{0:T(1024)S(1)} %get-tuple-element.48), channel_id=1, replica_groups=mesh['shard'=128,'tensor'=4] {'shard'}, use_global_device_ids=true, to_apply=%region_5.8 | all-reduce | flops 7680 | bytes 61440 | tf_op jit(solution)/shard_map/psum | solution.py:64
  2085.6 1.0 convolution_multiply_fusion.1
  2086.6 0.9 fusion.17
  2087.5 1.0 convolution_multiply_fusion
  2088.6 1.0 copy.52
  2089.6 0.6 multiply_subtract_fusion
  2090.2 53.0 %all_gather.10 = f32[128,1024]{0,1:T(8,128)S(1)} all-gather(f32[128,8]{0,1:T(8,128)S(1)} %get-tuple-element.44), channel_id=1, replica_groups=mesh['shard'=128,'tensor'=4] {'shard'}, dimensions={1}, use_global_device_ids=true | all-gather | bytes 528384 | tf_op jit(solution)/shard_map/all_gather | solution.py:89
  2143.3 1.0 copy.53
  2144.3 0.6 multiply_subtract_fusion.1
  2144.9 50.9 %all_gather.9 = f32[1024,128]{1,0:T(8,128)S(1)} all-gather(f32[8,128]{1,0:T(8,128)S(1)} %get-tuple-element.46), channel_id=1, replica_groups=mesh['shard'=128,'tensor'=4] {'shard'}, dimensions={0}, use_global_device_ids=true | all-gather | bytes 528384 | tf_op jit(solution)/shard_map/all_gather | solution.py:88
  2195.8 0.8 copy.63
  (54 shorter events, 2.0 us)
Async XLA Ops:
  7.2 1.5 copy-start
  7.2 1.2 copy-start.5
  7.2 790.8 %all-reduce.10.cloned.1.call-start = ((), (), s32[]{:S(2)}) async-start(), calls=%async_computation.1 | async-start | bytes 524288 | tf_op jit(solution)/shard_map/psum | solution.py:58
  520.6 8.3 copy-start.1
  527.6 1.3 copy-start.2
  527.6 1.3 copy-start.7
  530.3 1058.7 %all-reduce.8.cloned.1.call-start = ((), (), s32[]{:S(2)}) async-start(), calls=%async_computation | async-start | bytes 524288 | tf_op jit(solution)/shard_map/psum | solution.py:58
  530.3 1.9 copy-start.8
  798.0 1.4 copy-start.3
  1317.2 0.7 copy-start.13
  1317.2 0.7 copy-start.14
  1590.2 6.8 copy-start.4
  2086.6 0.9 copy-start.6
  2088.6 1.0 copy-start.9
  2088.6 1.0 copy-start.10
  2143.3 1.0 copy-start.11
  2143.3 1.0 copy-start.12
Sparse Core Ops, SparseCore 0:
  530.4 267.5 all-reduce.9
  1317.3 271.6 all-reduce.7
where the time goes:
time: 2200 us
  blocking collectives  1600 us (73%)
  waiting for transfers between devices  536 us (24%)
  other arithmetic  29.5 us (1%)
    psum x2, blocking collectives, local(): factor_query = lax.psum(right_query_part, 'shard')  976 us
    psum x2, waiting for transfers between devices, local(): sum_query = lax.psum(part_query, ('shard', 'tensor'))  536 us
    psum x1, blocking collectives, local(): sum_output = lax.psum(part_output, 'shard')  498 us
    all_gather x1, blocking collectives, local(): lax.all_gather(stepped_output, 'shard', axis=1, tiled=True)  53 us
    all_gather x1, blocking collectives, local(): lax.all_gather(stepped_query, 'shard', axis=0, tiled=True)  50.9 us
  transfers between devices with their start and end apart: 2, of which 2 were waited for; matrix products, arithmetic and copies ran while one was open for 0% of the time, Pallas kernels for 0%

commit v1 on v0

--- a/solution.py
+++ b/solution.py
@@ -55,7 +55,8 @@
     for turn in range(ROUNDS):
         part_query = product(total_query, factor_query)
         part_output = product(total_output, factor_output)
-        sum_query = lax.psum(part_query, ("shard", "tensor"))
+        one_axis = lax.psum(part_query, "shard")
+        sum_query = lax.psum(one_axis, "tensor")
         sum_output = lax.psum(part_output, "shard")
         left_query = orthonormal(sum_query)
         left_output = orthonormal_rows(sum_output)

time: 2200 us -> 2100 us (0.955)
  blocking collectives: 1600 us -> 1110 us
  waiting for transfers between devices: 536 us -> 923 us
    psum x1 -> x0, blocking collectives: 498 us -> none  [local(): sum_output = lax.psum(part_output, 'shard')]
    psum x2 -> x6, waiting for transfers between devices: 536 us -> 923 us  [the longest x2 466 us: local(): factor_output = lax.psum(right_output_part, ('shard', 'tensor'))]
  transfers between devices with their start and end apart: 2 -> 6, of which waited for: 2 -> 6; matrix products, arithmetic and copies ran while one was open for 0% -> 0% of each run, Pallas kernels for 0% -> 0%
where the time goes in v1:
time: 2100 us
  blocking collectives  1110 us (53%)
  waiting for transfers between devices  923 us (44%)
  other arithmetic  29.5 us (1%)
    psum x2, blocking collectives, local(): factor_query = lax.psum(right_query_part, 'shard')  983 us
    psum x2, waiting for transfers between devices, local(): factor_output = lax.psum(right_output_part, ('shard', 'tensor'))  466 us
    psum x2, waiting for transfers between devices, local(): one_axis = lax.psum(part_query, 'shard')  369 us
    psum x2, waiting for transfers between devices, local(): sum_query = lax.psum(one_axis, 'tensor')  87.5 us
    all_gather x1, blocking collectives, local(): lax.all_gather(stepped_query, 'shard', axis=0, tiled=True)  55.5 us
    all_gather x1, blocking collectives, local(): lax.all_gather(stepped_output, 'shard', axis=1, tiled=True)  49 us
  transfers between devices with their start and end apart: 6, of which 6 were waited for; matrix products, arithmetic and copies ran while one was open for 0% of the time, Pallas kernels for 0%

profile of v1, /device:TPU:1, one launch (start us, length us, event | category | flops | bytes accessed | tf_op | source)
XLA Modules:
  0.0 2103.3 jit_solution(4282501225335525313)
XLA Ops:
  7.2 2.5 fusion.15
  10.0 0.8 copy-done.4
  11.0 189.1 %all-reduce.10.cloned.1.call-done = f32[1024,32]{0,1:T(8,128)} async-done(((f32[1024,32]{0,1:T(8,128)}), f32[1024,32]{0,1:T(8,128)}) %all-reduce.10.cloned.1.call-update) | async-done | bytes 131088 | tf_op jit(solution)/shard_map/psum | solution.py:58
  200.6 1.3 dynamic-slice
  202.6 43.5 %all-reduce.12.cloned.1.call-done = f32[1024,32]{0,1:T(8,128)} async-done(((f32[1024,32]{0,1:T(8,128)}), f32[1024,32]{0,1:T(8,128)}) %all-reduce.12.cloned.1.call-update) | async-done | bytes 131088 | tf_op jit(solution)/shard_map/psum | solution.py:59
  246.1 1.2 fusion.40
  247.5 2.9 cholesky.74
  250.4 0.6 compare_reduce_fusion.3
  251.1 0.7 fusion.22
  251.7 2.4 custom-call.10
  254.1 1.2 fusion.20
  255.9 491.5 %all-reduce.2 = (f32[128,32]{0,1:T(8,128)S(1)}, f32[128,32]{0,1:T(8,128)S(1)}, f32[3584]{0:T(1024)S(1)}) all-reduce(f32[128,32]{0,1:T(8,128)S(1)} %fusion.13, f32[128,32]{0,1:T(8,128)S(1)} %fusion.6, f32[3584]{0:T(1024)S(1)} %convert_reduce_fusion), channel_id=1, replica_groups=mesh['shard'=128,'tensor'=4] {'shard'}, use_global_device_ids=true, to_apply=%region_4.7 | all-reduce | flops 11776 | bytes 94208 | tf_op jit(solution)/shard_map/psum | solution.py:65
  747.6 12.3 psum.98
  759.9 2.9 cholesky.96
  762.9 0.6 compare_reduce_fusion.1
  763.5 0.7 fusion.24
  764.2 2.4 custom-call.12
  766.9 1.3 fusion.11
  768.2 1.3 fusion.4
  769.7 0.6 copy-done.11
  770.3 0.6 subtract_dynamic-update-slice_fusion
  770.9 180.2 %all-reduce.14.cloned.1.call-done = f32[1024,32]{0,1:T(8,128)} async-done(((f32[1024,32]{0,1:T(8,128)}), f32[1024,32]{0,1:T(8,128)}) %all-reduce.14.cloned.1.call-update) | async-done | bytes 131088 | tf_op jit(solution)/shard_map/psum | solution.py:58
  951.1 261.9 %all-reduce.18.cloned.1.call-done = f32[1024,32]{0,1:T(8,128)} async-done(((f32[1024,32]{0,1:T(8,128)}), f32[1024,32]{0,1:T(8,128)}) %all-reduce.18.cloned.1.call-update) | async-done | bytes 131088 | tf_op jit(solution)/shard_map/psum | solution.py:66
  1213.0 1.3 fusion.2
  1214.4 44.0 %all-reduce.16.cloned.1.call-done = f32[1024,32]{0,1:T(8,128)} async-done(((f32[1024,32]{0,1:T(8,128)}), f32[1024,32]{0,1:T(8,128)}) %all-reduce.16.cloned.1.call-update) | async-done | bytes 131088 | tf_op jit(solution)/shard_map/psum | solution.py:59
  1258.4 1.2 fusion.41
  1259.7 2.9 cholesky.85
  1262.7 0.6 compare_reduce_fusion.2
  1263.3 0.7 fusion.23
  1264.0 2.4 custom-call.11
  1267.2 491.5 %all-reduce.1 = (f32[128,32]{0,1:T(8,128)S(1)}, f32[128,32]{0,1:T(8,128)S(1)}, f32[3584]{0:T(1024)}) all-reduce(f32[128,32]{0,1:T(8,128)S(1)} %fusion.9, f32[128,32]{0,1:T(8,128)S(1)} %fusion.2, f32[3584]{0:T(1024)S(1)} %get-tuple-element.45), channel_id=1, replica_groups=mesh['shard'=128,'tensor'=4] {'shard'}, use_global_device_ids=true, to_apply=%region_7.10 | all-reduce | flops 11776 | bytes 94208 | tf_op jit(solution)/shard_map/psum | solution.py:65
  1758.9 12.3 psum.101
  1771.3 2.9 cholesky.107
  1774.2 0.6 compare_reduce_fusion
  1774.9 0.7 fusion.25
  1775.5 2.4 custom-call.13
  1778.2 1.3 fusion
  1779.5 1.0 convolution_multiply_fusion.1
  1780.6 0.9 fusion.17
  1781.4 0.6 multiply_subtract_fusion.1
  1782.0 55.5 %all_gather.9 = f32[1024,128]{1,0:T(8,128)S(1)} all-gather(f32[8,128]{1,0:T(8,128)S(1)} %get-tuple-element.43), channel_id=1, replica_groups=mesh['shard'=128,'tensor'=4] {'shard'}, dimensions={0}, use_global_device_ids=true | all-gather | bytes 528384 | tf_op jit(solution)/shard_map/all_gather | solution.py:89
  1837.5 204.5 %all-reduce.20.cloned.1.call-done = f32[1024,32]{0,1:T(8,128)} async-done(((f32[1024,32]{0,1:T(8,128)}), f32[1024,32]{0,1:T(8,128)}) %all-reduce.20.cloned.1.call-update) | async-done | bytes 131088 | tf_op jit(solution)/shard_map/psum | solution.py:66
  2042.0 1.9 convolution_multiply_fusion
  2044.0 1.0 copy.52
  2045.0 0.6 multiply_subtract_fusion
  2045.6 49.0 %all_gather.10 = f32[128,1024]{0,1:T(8,128)S(1)} all-gather(f32[128,8]{0,1:T(8,128)S(1)} %get-tuple-element.41), channel_id=1, replica_groups=mesh['shard'=128,'tensor'=4] {'shard'}, dimensions={1}, use_global_device_ids=true | all-gather | bytes 528384 | tf_op jit(solution)/shard_map/all_gather | solution.py:90
  2094.6 1.0 copy.53
  2095.6 0.8 copy.65
  (61 shorter events, 3.8 us)
Async XLA Ops:
  7.2 192.9 %copy-start = (f32[1024,32]{0,1:T(8,128)S(1)}, f32[1024,32]{0,1:T(8,128)}, u32[]{:S(2)}) copy-start(f32[1024,32]{0,1:T(8,128)} %param.23) | copy-start | bytes 393220
  7.2 192.8 %all-reduce.10.cloned.1.call-start = ((), (), s32[]{:S(2)}) async-start(), calls=%async_computation | async-start | bytes 262144 | tf_op jit(solution)/shard_map/psum | solution.py:58
  7.2 2.6 copy-start.5
  9.7 1.0 copy-start.4
  9.7 236.4 %all-reduce.12.cloned.1.call-start = ((), (), s32[]{:S(2)}) async-start(), calls=%async_computation.1 | async-start | bytes 262144 | tf_op jit(solution)/shard_map/psum | solution.py:59
  200.1 751.0 %all-reduce.14.cloned.1.call-start = ((), (), s32[]{:S(2)}) async-start(), calls=%async_computation.2 | async-start | bytes 262144 | tf_op jit(solution)/shard_map/psum | solution.py:58
  200.1 2.5 copy-start.6
  200.1 55.3 %copy-start.2 = (bf16[1,1024,128]{2,1,0:T(8,128)(2,1)S(1)}, bf16[1,1024,128]{2,1,0:T(8,128)(2,1)}, u32[]{:S(2)}) copy-start(bf16[1,1024,128]{2,1,0:T(8,128)(2,1)} %param.18) | copy-start | bytes 786436
  200.6 54.8 %copy-start.1 = (f32[1,1024,128]{2,1,0:T(8,128)S(1)}, f32[1,1024,128]{2,1,0:T(8,128)}, u32[]{:S(2)}) copy-start(f32[1,1024,128]{2,1,0:T(8,128)} %param.19) | copy-start | bytes 1572868
  768.2 444.9 %all-reduce.18.cloned.1.call-start = ((), (), s32[]{:S(2)}) async-start(), calls=%async_computation.4 | async-start | bytes 262144 | tf_op jit(solution)/shard_map/psum | solution.py:66
  769.6 488.8 %all-reduce.16.cloned.1.call-start = ((), (), s32[]{:S(2)}) async-start(), calls=%async_computation.3 | async-start | bytes 262144 | tf_op jit(solution)/shard_map/psum | solution.py:59
  769.6 0.7 copy-start.11
  769.6 0.7 copy-start.12
  951.1 1090.9 %all-reduce.20.cloned.1.call-start = ((), (), s32[]{:S(2)}) async-start(), calls=%async_computation.5 | async-start | bytes 262144 | tf_op jit(solution)/shard_map/psum | solution.py:66
  1259.6 6.8 copy-start.3
  1780.5 0.9 copy-start.7
  1780.6 0.9 copy-start.8
  2044.0 1.0 copy-start.9
  2044.0 1.0 copy-start.10
Sparse Core Ops, SparseCore 0:
  11.9 188.1 all-reduce.9
  202.3 43.7 all-reduce.11
  768.3 182.7 all-reduce.13
  957.3 255.7 all-reduce.17
  1215.2 43.1 all-reduce.15
  1779.7 262.2 all-reduce.19
